TPU v7x, 32 devices: a whole 2x2x4 slice. The times are simulated.
32 devices in a mesh: narrow: 4 (over z), wide: 8 (over y, x, core).
Axes of the slice: x: 2, y: 2, z: 4, core: 2. Of those that a mesh axis runs over, the one named last changes fastest.
Arguments:
- tokens: bfloat16 [12288, 640], P('wide'), may hold values from -6 to 6
- cotangent: bfloat16 [12288, 640], P('wide'), may hold values from -6 to 6
- seq_lens: int32 [8, 16], P('wide'), may hold values from 1 to 1024, 1536 in all within a row
- norm_gains: bfloat16 [2, 640], replicated, may hold values from 0.099609375 to 1.8984375
- norm_shifts: bfloat16 [2, 640], replicated, may hold values from -3 to 3
- w_qkv: bfloat16 [3, 640, 640], P(None, 'wide', 'narrow'), may hold values from -0.25 to 0.25
- w_attn_out: bfloat16 [640, 640], P('narrow', 'wide'), may hold values from -2 to 2
- w_ffn_in: bfloat16 [640, 5120], P('narrow', 'wide'), may hold values from -0.25 to 0.25
- w_ffn_down: bfloat16 [640, 5120], P('narrow', 'wide'), may hold values from -0.078125 to 0.078125
Outputs:
- layer_out: bfloat16 [12288, 640], P('wide')
- input_grad: bfloat16 [12288, 640], P('wide')
- grad_norm_gains: float32 [2, 640], P(None, 'wide')
- grad_norm_shifts: float32 [2, 640], P(None, 'wide')
- grad_qkv: float32 [3, 640, 640], P(None, 'wide', 'narrow')
- grad_attn_out: float32 [640, 640], P('narrow', 'wide')
- grad_ffn_in: float32 [640, 5120], P('narrow', 'wide')
- grad_ffn_down: float32 [640, 5120], P('narrow', 'wide')
Inputs may be any that keep to these rules, and one draw needn't show every extreme that they name: `seq_lens`: each row lists the lengths of the 16 sequences packed end to end in that index's 1536 slots; a row sums to 1536 and its largest entry is exactly 1024.
All inputs are finite; a program needn't handle non-finite values.
Results may differ from a plain program's by a relative error of at most 0.015.
Values may be sent and summed in bfloat16 or wider, within the bound.
No kernel may reach another device: no remote copies, remote signals or barrier semaphores. Data moves between devices by JAX's collectives and lax.ppermute only.
A program may use at most 128 MiB of HBM per device.

v0:
```python
from functools import partial
import jax
import jax.numpy as jnp
from jax import lax
from jax.sharding import PartitionSpec as P

HD = 32
QBLK = 512
FBLK = 128
EPS = 1e-05


def layer_norm(rows, gain, shift):
    center = rows - jnp.mean(rows, axis=-1, keepdims=True)
    spread = jnp.mean(center * center, axis=-1, keepdims=True)
    return center * lax.rsqrt(spread + EPS) * gain + shift


def segment_ids(lengths, count):
    ends = jnp.cumsum(lengths, dtype=jnp.int32)
    position = jnp.arange(count, dtype=jnp.int32)
    return jnp.sum((position[:, None] >= ends[None, :]).astype(jnp.int32), axis=1)


def block_scores(q_block, keys, seg_block, segment):
    scores = jnp.einsum("qd,kd->qk", q_block, keys, preferred_element_type=jnp.float32) * HD ** (
        -0.5
    )
    return jnp.where(seg_block[:, None] == segment[None, :], scores, -1e30)


def attend_forward(query, key, value, segment):
    count, width = query.shape
    starts = jnp.arange(count // QBLK, dtype=jnp.int32) * QBLK

    def one_head(head):
        q_head = lax.dynamic_slice_in_dim(query, head * HD, HD, 1)
        k_head = lax.dynamic_slice_in_dim(key, head * HD, HD, 1)
        v_head = lax.dynamic_slice_in_dim(value, head * HD, HD, 1)

        def one_block(start):
            q_block = lax.dynamic_slice_in_dim(q_head, start, QBLK, 0)
            seg_block = lax.dynamic_slice_in_dim(segment, start, QBLK, 0)
            scores = block_scores(q_block, k_head, seg_block, segment)
            top = jnp.max(scores, axis=1, keepdims=True)
            expd = jnp.exp(scores - top)
            total = jnp.sum(expd, axis=1, keepdims=True)
            weights = (expd / total).astype(jnp.bfloat16)
            result = jnp.dot(weights, v_head, preferred_element_type=jnp.float32)
            return (result, (top + jnp.log(total))[:, 0])

        results, logsum = lax.map(one_block, starts)
        return (results.reshape(count, HD), logsum.reshape(count))

    results, logsum = lax.map(one_head, jnp.arange(width // HD, dtype=jnp.int32))
    return (results.transpose(1, 0, 2).reshape(count, width), logsum)


def attend_backward(query, key, value, dattended, logsum, segment):
    count, width = query.shape
    starts = jnp.arange(count // QBLK, dtype=jnp.int32) * QBLK
    scale = HD ** (-0.5)

    def one_head(head):
        q_head = lax.dynamic_slice_in_dim(query, head * HD, HD, 1)
        k_head = lax.dynamic_slice_in_dim(key, head * HD, HD, 1)
        v_head = lax.dynamic_slice_in_dim(value, head * HD, HD, 1)
        d_head = lax.dynamic_slice_in_dim(dattended, head * HD, HD, 1)
        log_head = logsum[head]

        def one_block(carry, start):
            dkey, dvalue = carry
            q_block = lax.dynamic_slice_in_dim(q_head, start, QBLK, 0)
            d_block = lax.dynamic_slice_in_dim(d_head, start, QBLK, 0)
            seg_block = lax.dynamic_slice_in_dim(segment, start, QBLK, 0)
            log_block = lax.dynamic_slice_in_dim(log_head, start, QBLK, 0)
            scores = block_scores(q_block, k_head, seg_block, segment)
            prob = jnp.exp(scores - log_block[:, None])
            dprob = jnp.einsum("qd,kd->qk", d_block, v_head, preferred_element_type=jnp.float32)
            delta = jnp.sum(prob * dprob, axis=1, keepdims=True)
            dscore = (prob * (dprob - delta)).astype(jnp.bfloat16)
            dquery = jnp.dot(dscore, k_head, preferred_element_type=jnp.float32) * scale
            dkey = (
                dkey
                + jnp.einsum("qk,qd->kd", dscore, q_block, preferred_element_type=jnp.float32)
                * scale
            )
            dvalue = dvalue + jnp.einsum(
                "qk,qd->kd", prob.astype(jnp.bfloat16), d_block, preferred_element_type=jnp.float32
            )
            return ((dkey, dvalue), dquery)

        zeros = jnp.zeros((count, HD), jnp.float32)
        (dkey, dvalue), dquery = lax.scan(one_block, (zeros, zeros), starts)
        return (dquery.reshape(count, HD), dkey, dvalue)

    dquery, dkey, dvalue = lax.map(one_head, jnp.arange(width // HD, dtype=jnp.int32))

    def joined(arr):
        return arr.transpose(1, 0, 2).reshape(count, width)

    return (joined(dquery), joined(dkey), joined(dvalue))


def hidden_block(normed_mine, ffn_in_full, start):
    x_block = lax.dynamic_slice_in_dim(normed_mine, start, FBLK, 0)
    share = lax.psum_scatter(
        jnp.dot(x_block, ffn_in_full, preferred_element_type=jnp.float32),
        "narrow",
        scatter_dimension=0,
        tiled=True,
    )
    act_share = jax.nn.gelu(share, approximate=False).astype(jnp.bfloat16)
    act_rows = lax.all_gather(act_share, "narrow", axis=0, tiled=True)
    return (x_block, share, act_rows)


def local(
    tokens, cotangent, seq_lens, norm_gains, norm_shifts, w_qkv, w_attn_out, w_ffn_in, w_ffn_down
):
    count = tokens.shape[0]
    width = w_attn_out.shape[0]
    first_col = lax.axis_index("narrow") * width
    gains = norm_gains.astype(jnp.float32)
    shifts = norm_shifts.astype(jnp.float32)
    segment = segment_ids(seq_lens[0], count)
    resid = tokens.astype(jnp.float32)
    dy_full = cotangent.astype(jnp.float32)
    qkv_full, out_full = (
        lax.all_gather(w_qkv, "wide", axis=1, tiled=True),
        lax.all_gather(w_attn_out, "wide", axis=1, tiled=True),
    )
    normed_low = layer_norm(resid, gains[0], shifts[0]).astype(jnp.bfloat16)
    proj = jnp.einsum(
        "td,jde->jte", normed_low, qkv_full, preferred_element_type=jnp.float32
    ).astype(jnp.bfloat16)
    query, key, value = (proj[0], proj[1], proj[2])
    attended, logsum = attend_forward(query, key, value, segment)
    attended_low = attended.astype(jnp.bfloat16)
    mixed = jnp.dot(attended_low, out_full, preferred_element_type=jnp.float32)
    mixed_mine = lax.psum_scatter(mixed, "narrow", scatter_dimension=1, tiled=True)
    middle_mine = lax.dynamic_slice_in_dim(resid, first_col, width, 1) + mixed_mine
    middle = lax.all_gather(middle_mine, "narrow", axis=1, tiled=True)
    normed_two = layer_norm(middle, gains[1], shifts[1])
    ffn_in_part, ffn_down_part = (
        lax.all_gather(w_ffn_in, "wide", axis=1, tiled=True),
        lax.all_gather(w_ffn_down, "wide", axis=1, tiled=True),
    )
    dy_cols = lax.dynamic_slice_in_dim(cotangent, first_col, width, 1)
    normed_mine = lax.dynamic_slice_in_dim(normed_two, first_col, width, 1).astype(jnp.bfloat16)
    starts = jnp.arange(count // FBLK, dtype=jnp.int32) * FBLK

    def ffn_forward(carry, start):
        x_block, share, act_rows = hidden_block(normed_mine, ffn_in_part, start)
        result = lax.dot_general(
            act_rows, ffn_down_part, (((1,), (1,)), ((), ())), preferred_element_type=jnp.float32
        )
        return (carry, result)

    _, branch = lax.scan(ffn_forward, jnp.zeros((), jnp.float32), starts)
    branch_full = lax.all_gather(
        branch.reshape(count, width).astype(jnp.bfloat16), "narrow", axis=1, tiled=True
    ).astype(jnp.float32)
    layer_out = (middle + branch_full).astype(jnp.bfloat16)

    def ffn_backward(carry, start):
        grad_in, grad_down = carry
        x_block, share, act_rows = hidden_block(normed_mine, ffn_in_part, start)
        dy_block = lax.dynamic_slice_in_dim(dy_cols, start, FBLK, 0)
        dact = lax.psum_scatter(
            jnp.dot(dy_block, ffn_down_part, preferred_element_type=jnp.float32),
            "narrow",
            scatter_dimension=0,
            tiled=True,
        )
        _, gelu_back = jax.vjp(partial(jax.nn.gelu, approximate=False), share)
        dshare = gelu_back(dact)[0].astype(jnp.bfloat16)
        drows = lax.all_gather(dshare, "narrow", axis=0, tiled=True)
        grad_in = grad_in + lax.dot_general(
            x_block, drows, (((0,), (0,)), ((), ())), preferred_element_type=jnp.float32
        )
        grad_down = grad_down + lax.dot_general(
            dy_block, act_rows, (((0,), (0,)), ((), ())), preferred_element_type=jnp.float32
        )
        dnormed = lax.dot_general(
            drows, ffn_in_part, (((1,), (1,)), ((), ())), preferred_element_type=jnp.float32
        )
        return ((grad_in, grad_down), dnormed)

    empty = jnp.zeros(ffn_in_part.shape, jnp.float32)
    (grad_in, grad_down), dnormed = lax.scan(ffn_backward, (empty, empty), starts)
    dnormed_two = lax.all_gather(dnormed.reshape(count, width), "narrow", axis=1, tiled=True)
    grad_in_out, grad_down_out = (
        lax.psum_scatter(grad_in, "wide", scatter_dimension=1, tiled=True),
        lax.psum_scatter(grad_down, "wide", scatter_dimension=1, tiled=True),
    )
    _, norm_back_two = jax.vjp(layer_norm, middle, gains[1], shifts[1])
    dmiddle, dgain_two, dshift_two = norm_back_two(dnormed_two)
    dmiddle = dmiddle + dy_full
    dmixed_low = dmiddle.astype(jnp.bfloat16)
    grad_out = lax.dot_general(
        attended_low, dmixed_low, (((0,), (0,)), ((), ())), preferred_element_type=jnp.float32
    )
    dattended = lax.dot_general(
        dmixed_low, out_full, (((1,), (1,)), ((), ())), preferred_element_type=jnp.float32
    ).astype(jnp.bfloat16)
    dquery, dkey, dvalue = attend_backward(query, key, value, dattended, logsum, segment)
    dproj = jnp.stack([dquery, dkey, dvalue]).astype(jnp.bfloat16)
    grad_proj = jnp.einsum("td,jte->jde", normed_low, dproj, preferred_element_type=jnp.float32)
    dnormed_part = jnp.einsum("jte,jde->td", dproj, qkv_full, preferred_element_type=jnp.float32)
    dnormed_one = lax.psum(dnormed_part.astype(jnp.bfloat16), "narrow").astype(jnp.float32)
    _, norm_back_one = jax.vjp(layer_norm, resid, gains[0], shifts[0])
    dresid, dgain_one, dshift_one = norm_back_one(dnormed_one)
    input_grad = (dmiddle + dresid).astype(jnp.bfloat16)
    dgains = jnp.stack([dgain_one, dgain_two])
    dshifts = jnp.stack([dshift_one, dshift_two])
    gain_out, shift_out, proj_out, attn_out = (
        lax.psum_scatter(dgains, "wide", scatter_dimension=1, tiled=True),
        lax.psum_scatter(dshifts, "wide", scatter_dimension=1, tiled=True),
        lax.psum_scatter(grad_proj, "wide", scatter_dimension=1, tiled=True),
        lax.psum_scatter(grad_out, "wide", scatter_dimension=1, tiled=True),
    )
    return (
        layer_out,
        input_grad,
        gain_out,
        shift_out,
        proj_out,
        attn_out,
        grad_in_out,
        grad_down_out,
    )


def solution(mesh):
    placed = (
        P("wide", None),
        P("wide", None),
        P("wide", None),
        P(),
        P(),
        P(None, "wide", "narrow"),
        P("narrow", "wide"),
        P("narrow", "wide"),
        P("narrow", "wide"),
    )
    return jax.shard_map(
        local,
        mesh=mesh,
        in_specs=placed,
        out_specs=(
            P("wide", None),
            P("wide", None),
            P(None, "wide"),
            P(None, "wide"),
            P(None, "wide", "narrow"),
            P("narrow", "wide"),
            P("narrow", "wide"),
            P("narrow", "wide"),
        ),
        check_vma=False,
    )
```

profile of v0, /device:TPU:0, one launch (start us, length us, event | category | flops | bytes accessed | tf_op | source)
XLA Modules:
  0.0 4609.1 jit_solution(13928919483076880924)
XLA Ops:
  36.1 182.4 %while.84 = (s32[]{:T(128)}, bf16[5,1536,32]{1,2,0:T(8,128)(2,1)}, f32[5,1536]{1,0:T(8,128)}, s32[5]{0:T(128)}, bf16[1536,160]{1,0:T(8,128)(2,1)}, /*index=5*/bf...) while((s32[]{:T(128)}, bf16[5,1536,32]{1,2,0:T(8,128)(2,1)}, ...), condition=%wide.region_9.10_spmd.clone, body=%wide.region_4.9_spmd.clone.sunk | while | flops 107740680 | bytes 11363814 | solution.py:55
  236.6 69.2 %reduce-scatter.19.cloned.1.call-done = f32[1536,160]{0,1:T(8,128)} async-done(((f32[1536,640]{0,1:T(8,128)}), f32[1536,160]{0,1:T(8,128)}) %reduce-scatter.19.cloned.1.call-update) | async-done | bytes 983056 | tf_op jit(solution)/shard_map/reduce_scatter | solution.py:141
  312.1 73.2 %all-gather.9.cloned.1.call-done = f32[1536,640]{0,1:T(8,128)} async-done(((f32[1536,160]{0,1:T(8,128)}), f32[1536,640]{0,1:T(8,128)}) %all-gather.9.cloned.1.call-update) | async-done | bytes 3932176 | tf_op jit(solution)/shard_map/all_gather | solution.py:143
  439.6 2218.3 %while.87 = (s32[]{:T(128)}, f32[160,5120]{1,0:T(8,128)}, f32[160,5120]{1,0:T(8,128)}, f32[12,128,160]{1,0,2:T(8,128)}, s32[12]{0:T(128)S(1)}, /*index=5*/bf16[1...) while((s32[]{:T(128)}, f32[160,5120]{1,0:T(8,128)}, ...), condition=%wide.region_19.20_spmd.clone, body=%wide.region_16.19_spmd.clone.sunk | while | flops 1064796160 | bytes 83411448 | solution.py:191
  1239.3 50.9 %reduce-scatter.35.cloned.1.call-done = f32[32,5120]{1,0:T(8,128)} async-done(((f32[128,5120]{1,0:T(8,128)}), f32[32,5120]{1,0:T(8,128)}) %reduce-scatter.35.cloned.1.call-update) | async-done | bytes 655376 | tf_op jit(solution)/shard_map/while/body/eval_jaxpr/reduce_scatter | solution.py:170
  1794.0 50.9 %reduce-scatter.35.cloned.1.call-done = f32[32,5120]{1,0:T(8,128)} async-done(((f32[128,5120]{1,0:T(8,128)}), f32[32,5120]{1,0:T(8,128)}) %reduce-scatter.35.cloned.1.call-update) | async-done | bytes 655376 | tf_op jit(solution)/shard_map/while/body/eval_jaxpr/reduce_scatter | solution.py:170
  2163.8 50.9 %reduce-scatter.35.cloned.1.call-done = f32[32,5120]{1,0:T(8,128)} async-done(((f32[128,5120]{1,0:T(8,128)}), f32[32,5120]{1,0:T(8,128)}) %reduce-scatter.35.cloned.1.call-update) | async-done | bytes 655376 | tf_op jit(solution)/shard_map/while/body/eval_jaxpr/reduce_scatter | solution.py:170
  2533.6 50.9 %reduce-scatter.35.cloned.1.call-done = f32[32,5120]{1,0:T(8,128)} async-done(((f32[128,5120]{1,0:T(8,128)}), f32[32,5120]{1,0:T(8,128)}) %reduce-scatter.35.cloned.1.call-update) | async-done | bytes 655376 | tf_op jit(solution)/shard_map/while/body/eval_jaxpr/reduce_scatter | solution.py:170
  2660.5 1148.4 %while.82 = (s32[]{:T(128)}, bf16[12,128,160]{1,2,0:T(8,128)(2,1)}, s32[12]{0:T(128)S(1)}, bf16[1536,160]{1,0:T(8,128)(2,1)}, bf16[160,5120]{1,0:T(8,128)(2,1)},...) while((s32[]{:T(128)}, bf16[12,128,160]{1,2,0:T(8,128)(2,1)}, s32[12]{0:T(128)S(1)}, ...), condition=%wide.region_15.16_spmd, body=%wide.region_13.15_spmd.sunk | while | flops 430080000 | bytes 29638920 | solution.py:160
  2666.7 51.2 %reduce-scatter.33.cloned.1.call-done = f32[32,5120]{1,0:T(8,128)} async-done(((f32[128,5120]{1,0:T(8,128)}), f32[32,5120]{1,0:T(8,128)}) %reduce-scatter.33.cloned.1.call-update) | async-done | bytes 655376 | tf_op jit(solution)/shard_map/while/body/eval_jaxpr/reduce_scatter | solution.py:107
  2762.4 51.2 %reduce-scatter.33.cloned.1.call-done = f32[32,5120]{1,0:T(8,128)} async-done(((f32[128,5120]{1,0:T(8,128)}), f32[32,5120]{1,0:T(8,128)}) %reduce-scatter.33.cloned.1.call-update) | async-done | bytes 655376 | tf_op jit(solution)/shard_map/while/body/eval_jaxpr/reduce_scatter | solution.py:107
  2858.2 51.2 %reduce-scatter.33.cloned.1.call-done = f32[32,5120]{1,0:T(8,128)} async-done(((f32[128,5120]{1,0:T(8,128)}), f32[32,5120]{1,0:T(8,128)}) %reduce-scatter.33.cloned.1.call-update) | async-done | bytes 655376 | tf_op jit(solution)/shard_map/while/body/eval_jaxpr/reduce_scatter | solution.py:107
  2953.9 51.2 %reduce-scatter.33.cloned.1.call-done = f32[32,5120]{1,0:T(8,128)} async-done(((f32[128,5120]{1,0:T(8,128)}), f32[32,5120]{1,0:T(8,128)}) %reduce-scatter.33.cloned.1.call-update) | async-done | bytes 655376 | tf_op jit(solution)/shard_map/while/body/eval_jaxpr/reduce_scatter | solution.py:107
  3049.6 51.2 %reduce-scatter.33.cloned.1.call-done = f32[32,5120]{1,0:T(8,128)} async-done(((f32[128,5120]{1,0:T(8,128)}), f32[32,5120]{1,0:T(8,128)}) %reduce-scatter.33.cloned.1.call-update) | async-done | bytes 655376 | tf_op jit(solution)/shard_map/while/body/eval_jaxpr/reduce_scatter | solution.py:107
  3145.3 51.2 %reduce-scatter.33.cloned.1.call-done = f32[32,5120]{1,0:T(8,128)} async-done(((f32[128,5120]{1,0:T(8,128)}), f32[32,5120]{1,0:T(8,128)}) %reduce-scatter.33.cloned.1.call-update) | async-done | bytes 655376 | tf_op jit(solution)/shard_map/while/body/eval_jaxpr/reduce_scatter | solution.py:107
  3241.0 51.2 %reduce-scatter.33.cloned.1.call-done = f32[32,5120]{1,0:T(8,128)} async-done(((f32[128,5120]{1,0:T(8,128)}), f32[32,5120]{1,0:T(8,128)}) %reduce-scatter.33.cloned.1.call-update) | async-done | bytes 655376 | tf_op jit(solution)/shard_map/while/body/eval_jaxpr/reduce_scatter | solution.py:107
  3336.7 51.2 %reduce-scatter.33.cloned.1.call-done = f32[32,5120]{1,0:T(8,128)} async-done(((f32[128,5120]{1,0:T(8,128)}), f32[32,5120]{1,0:T(8,128)}) %reduce-scatter.33.cloned.1.call-update) | async-done | bytes 655376 | tf_op jit(solution)/shard_map/while/body/eval_jaxpr/reduce_scatter | solution.py:107
  3432.4 51.2 %reduce-scatter.33.cloned.1.call-done = f32[32,5120]{1,0:T(8,128)} async-done(((f32[128,5120]{1,0:T(8,128)}), f32[32,5120]{1,0:T(8,128)}) %reduce-scatter.33.cloned.1.call-update) | async-done | bytes 655376 | tf_op jit(solution)/shard_map/while/body/eval_jaxpr/reduce_scatter | solution.py:107
  3528.1 51.2 %reduce-scatter.33.cloned.1.call-done = f32[32,5120]{1,0:T(8,128)} async-done(((f32[128,5120]{1,0:T(8,128)}), f32[32,5120]{1,0:T(8,128)}) %reduce-scatter.33.cloned.1.call-update) | async-done | bytes 655376 | tf_op jit(solution)/shard_map/while/body/eval_jaxpr/reduce_scatter | solution.py:107
  3623.8 51.2 %reduce-scatter.33.cloned.1.call-done = f32[32,5120]{1,0:T(8,128)} async-done(((f32[128,5120]{1,0:T(8,128)}), f32[32,5120]{1,0:T(8,128)}) %reduce-scatter.33.cloned.1.call-update) | async-done | bytes 655376 | tf_op jit(solution)/shard_map/while/body/eval_jaxpr/reduce_scatter | solution.py:107
  3719.5 51.2 %reduce-scatter.33.cloned.1.call-done = f32[32,5120]{1,0:T(8,128)} async-done(((f32[128,5120]{1,0:T(8,128)}), f32[32,5120]{1,0:T(8,128)}) %reduce-scatter.33.cloned.1.call-update) | async-done | bytes 655376 | tf_op jit(solution)/shard_map/while/body/eval_jaxpr/reduce_scatter | solution.py:107
  3814.6 72.3 %all-gather.17.cloned.1.call-done = f32[1536,640]{0,1:T(8,128)} async-done(((f32[1536,160]{0,1:T(8,128)}), f32[1536,640]{0,1:T(8,128)}) %all-gather.17.cloned.1.call-update) | async-done | bytes 3932176 | tf_op jit(solution)/shard_map/all_gather | solution.py:192
  3942.7 319.0 %while.86 = (s32[]{:T(128)}, bf16[5,1536,32]{2,1,0:T(8,128)(2,1)}, bf16[5,1536,32]{1,2,0:T(8,128)(2,1)}, bf16[5,1536,32]{1,2,0:T(8,128)(2,1)}, s32[5]{0:T(128)},...) while((s32[]{:T(128)}, bf16[5,1536,32]{2,1,0:T(8,128)(2,1)}, ...), condition=%wide.region_26.27_spmd.clone, body=%wide.region_22.26_spmd.clone.sunk | while | flops 259784208 | bytes 27660404 | solution.py:97
  4281.8 67.5 %all-reduce.2.cloned.1.call-done = bf16[1536,640]{0,1:T(8,128)(2,1)} async-done(((bf16[1536,640]{0,1:T(8,128)(2,1)}), bf16[1536,640]{0,1:T(8,128)(2,1)}) %all-reduce.2.cloned.1.call-update) | async-done | bytes 1966096 | tf_op jit(solution)/shard_map/psum | solution.py:211
  (1048 shorter events, 3746.6 us)
Async XLA Ops:
  7.2 298.6 %reduce-scatter.19.cloned.1.call-start = ((), (), s32[]{:S(2)}) async-start(), calls=%async_computation.10 | async-start | bytes 4915200 | tf_op jit(solution)/shard_map/reduce_scatter | solution.py:141
  232.6 152.7 %all-gather.9.cloned.1.call-start = ((), (), s32[]{:S(2)}) async-start(), calls=%async_computation.11 | async-start | bytes 4915200 | tf_op jit(solution)/shard_map/all_gather | solution.py:143
  309.1 130.5 %all-gather.13.cloned.1.call-start = ((), (), s32[]{:S(2)}) async-start(), calls=%async_computation.13 | async-start | bytes 1843200 | tf_op jit(solution)/shard_map/all_gather | solution.py:147
  445.8 106.3 %reduce-scatter.35.cloned.1.call-start = ((), (), s32[]{:S(2)}) async-start(), calls=%async_computation.25 | async-start | bytes 3276800 | tf_op jit(solution)/shard_map/while/body/eval_jaxpr/reduce_scatter | solution.py:170
  447.9 139.0 %all-gather.21.cloned.1.call-start = ((), (), s32[]{:S(2)}) async-start(), calls=%async_computation.27 | async-start | bytes 1638400 | tf_op jit(solution)/shard_map/while/body/eval_jaxpr/all_gather | solution.py:178
  632.8 138.0 %all-gather.21.cloned.1.call-start = ((), (), s32[]{:S(2)}) async-start(), calls=%async_computation.27 | async-start | bytes 1638400 | tf_op jit(solution)/shard_map/while/body/eval_jaxpr/all_gather | solution.py:178
  817.5 138.0 %all-gather.21.cloned.1.call-start = ((), (), s32[]{:S(2)}) async-start(), calls=%async_computation.27 | async-start | bytes 1638400 | tf_op jit(solution)/shard_map/while/body/eval_jaxpr/all_gather | solution.py:178
  1002.3 138.0 %all-gather.21.cloned.1.call-start = ((), (), s32[]{:S(2)}) async-start(), calls=%async_computation.27 | async-start | bytes 1638400 | tf_op jit(solution)/shard_map/while/body/eval_jaxpr/all_gather | solution.py:178
  1187.0 138.1 %all-gather.21.cloned.1.call-start = ((), (), s32[]{:S(2)}) async-start(), calls=%async_computation.27 | async-start | bytes 1638400 | tf_op jit(solution)/shard_map/while/body/eval_jaxpr/all_gather | solution.py:178
  1371.9 138.0 %all-gather.21.cloned.1.call-start = ((), (), s32[]{:S(2)}) async-start(), calls=%async_computation.27 | async-start | bytes 1638400 | tf_op jit(solution)/shard_map/while/body/eval_jaxpr/all_gather | solution.py:178
  1556.7 138.0 %all-gather.21.cloned.1.call-start = ((), (), s32[]{:S(2)}) async-start(), calls=%async_computation.27 | async-start | bytes 1638400 | tf_op jit(solution)/shard_map/while/body/eval_jaxpr/all_gather | solution.py:178
  1741.6 138.1 %all-gather.21.cloned.1.call-start = ((), (), s32[]{:S(2)}) async-start(), calls=%async_computation.27 | async-start | bytes 1638400 | tf_op jit(solution)/shard_map/while/body/eval_jaxpr/all_gather | solution.py:178
  1926.5 138.1 %all-gather.21.cloned.1.call-start = ((), (), s32[]{:S(2)}) async-start(), calls=%async_computation.27 | async-start | bytes 1638400 | tf_op jit(solution)/shard_map/while/body/eval_jaxpr/all_gather | solution.py:178
  2111.5 138.1 %all-gather.21.cloned.1.call-start = ((), (), s32[]{:S(2)}) async-start(), calls=%async_computation.27 | async-start | bytes 1638400 | tf_op jit(solution)/shard_map/while/body/eval_jaxpr/all_gather | solution.py:178
  2296.5 138.0 %all-gather.21.cloned.1.call-start = ((), (), s32[]{:S(2)}) async-start(), calls=%async_computation.27 | async-start | bytes 1638400 | tf_op jit(solution)/shard_map/while/body/eval_jaxpr/all_gather | solution.py:178
  2481.2 138.1 %all-gather.21.cloned.1.call-start = ((), (), s32[]{:S(2)}) async-start(), calls=%async_computation.27 | async-start | bytes 1638400 | tf_op jit(solution)/shard_map/while/body/eval_jaxpr/all_gather | solution.py:178
  3809.7 120.9 %all-gather.15.cloned.1.call-start = ((), (), s32[]{:S(2)}) async-start(), calls=%async_computation.14 | async-start | bytes 2457600 | tf_op jit(solution)/shard_map/all_gather | solution.py:161
  3811.6 537.6 %all-reduce.2.cloned.1.call-start = ((), (), s32[]{:S(2)}) async-start(), calls=%async_computation.16 | async-start | bytes 3932160 | tf_op jit(solution)/shard_map/psum | solution.py:211
  4268.3 117.7 %reduce-scatter.31.cloned.1.call-start = ((), (), s32[]{:S(2)}) async-start(), calls=%async_computation.22 | async-start | bytes 737280
  4271.6 155.6 %reduce-scatter.29.cloned.1.call-start = ((), (), s32[]{:S(2)}) async-start(), calls=%async_computation.21 | async-start | bytes 1474560
  4281.7 182.2 %reduce-scatter.27.cloned.1.call-start = ((), (), s32[]{:S(2)}) async-start(), calls=%async_computation.20 | async-start | bytes 368640
  4356.3 144.4 %reduce-scatter.25.cloned.1.call-start = ((), (), s32[]{:S(2)}) async-start(), calls=%async_computation.19 | async-start | bytes 368640
  4357.3 194.1 %reduce-scatter.21.cloned.1.call-start = ((), (), s32[]{:S(2)}) async-start(), calls=%async_computation.17 | async-start | bytes 3686400 | tf_op jit(solution)/shard_map/reduce_scatter | solution.py:194
  4357.9 244.4 %reduce-scatter.23.cloned.1.call-start = ((), (), s32[]{:S(2)}) async-start(), calls=%async_computation.18 | async-start | bytes 3686400 | tf_op jit(solution)/shard_map/reduce_scatter | solution.py:195
  (163 other events, 8291.0 us)
Sparse Core Ops, SparseCore 0:
  232.7 72.9 reduce-scatter.18
  308.5 76.8 all-gather.8
  445.9 52.0 reduce-scatter.36
  500.2 51.7 reduce-scatter.34
  684.1 51.7 reduce-scatter.34
  815.5 51.0 reduce-scatter.36
  868.8 51.7 reduce-scatter.34
  1000.3 51.0 reduce-scatter.36
  1053.6 51.7 reduce-scatter.34
  1238.4 51.7 reduce-scatter.34
  1369.9 51.0 reduce-scatter.36
  1423.2 51.7 reduce-scatter.34
  1608.0 51.7 reduce-scatter.34
  1739.6 51.0 reduce-scatter.36
  1793.1 51.7 reduce-scatter.34
  1977.9 51.7 reduce-scatter.34
  2162.9 51.7 reduce-scatter.34
  2294.5 51.1 reduce-scatter.36
  2347.8 51.7 reduce-scatter.34
  2532.7 51.7 reduce-scatter.34
  2666.8 51.1 reduce-scatter.32
  3336.7 51.0 reduce-scatter.32
  3811.4 75.4 all-gather.16
  4268.5 80.7 all-reduce.1
  (61 shorter events, 2296.3 us)
where the time goes:
time: 4630 us; the launch traced here: 4610 us
  waiting for transfers between devices  3470 us (75%)
  matrix products  501 us (11%)
  local copies, waits for them, and re-layouts  284 us (6%)
  other arithmetic  192 us (4%)
  loops' own time  119 us (3%)
    reduce_scatter x24, waiting for transfers between devices, hidden_block(): lax.psum_scatter(jnp.dot(x_block, ffn_in_full, preferred_element_type=jnp...  1200 us
    all_gather x24, waiting for transfers between devices, hidden_block(): act_rows = lax.all_gather(act_share, 'narrow', axis=0, tiled=True)  675 us
    reduce_scatter x12, waiting for transfers between devices, ffn_backward(): lax.psum_scatter(jnp.dot(dy_block, ffn_down_part, preferred_element_type=...  610 us
    all_gather x12, waiting for transfers between devices, ffn_backward(): drows = lax.all_gather(dshare, 'narrow', axis=0, tiled=True)  382 us
    unnamed x17, waiting for transfers between devices  126 us
  transfers between devices with their start and end apart: 85, of which 85 were waited for; matrix products, arithmetic and copies ran while one was open for 5% of the time, Pallas kernels for 0%

commit v1 on v0

--- a/solution.py
+++ b/solution.py
@@ -175,7 +175,16 @@
         )
         _, gelu_back = jax.vjp(partial(jax.nn.gelu, approximate=False), share)
         dshare = gelu_back(dact)[0].astype(jnp.bfloat16)
-        drows = lax.all_gather(dshare, "narrow", axis=0, tiled=True)
+        ring = [dshare]
+        for hop in range(3):
+            ring.append(
+                lax.ppermute(ring[-1], "narrow", [(dev, (dev + 1) % 4) for dev in range(4)])
+            )
+        drows = jnp.roll(
+            jnp.concatenate(ring[::-1], axis=0),
+            (lax.axis_index("narrow") + 1) * ring[0].shape[0],
+            axis=0,
+        )
         grad_in = grad_in + lax.dot_general(
             x_block, drows, (((0,), (0,)), ((), ())), preferred_element_type=jnp.float32
         )

time: 4630 us -> 4480 us (0.968)
  waiting for transfers between devices: 3470 us -> 3320 us
    all_gather x12 -> x0, waiting for transfers between devices: 382 us -> none  [ffn_backward(): drows = lax.all_gather(dshare, 'narrow', axis=0, tiled=True)]
    ppermute x0 -> x36, waiting for transfers between devices: none -> 358 us  [ffn_backward(): lax.ppermute(ring[-1], 'narrow', [(dev, (dev + 1) % 4) for dev in range(4)])]
    all_gather x24, waiting for transfers between devices: 675 us -> 567 us  [hidden_block(): act_rows = lax.all_gather(act_share, 'narrow', axis=0, tiled=True)]
  transfers between devices with their start and end apart: 85 -> 109, of which waited for: 85 -> 109; matrix products, arithmetic and copies ran while one was open for 5% -> 6% of each run, Pallas kernels for 0% -> 0%
where the time goes in v1:
time: 4480 us; the launch traced here: 4470 us
  waiting for transfers between devices  3320 us (74%)
  matrix products  476 us (11%)
  local copies, waits for them, and re-layouts  318 us (7%)
  other arithmetic  183 us (4%)
  loops' own time  119 us (3%)
    reduce_scatter x24, waiting for transfers between devices, hidden_block(): lax.psum_scatter(jnp.dot(x_block, ffn_in_full, preferred_element_type=jnp...  1190 us
    reduce_scatter x12, waiting for transfers between devices, ffn_backward(): lax.psum_scatter(jnp.dot(dy_block, ffn_down_part, preferred_element_type=...  610 us
    all_gather x24, waiting for transfers between devices, hidden_block(): act_rows = lax.all_gather(act_share, 'narrow', axis=0, tiled=True)  567 us
    ppermute x36, waiting for transfers between devices, ffn_backward(): lax.ppermute(ring[-1], 'narrow', [(dev, (dev + 1) % 4) for dev in range(4)])  358 us
    unnamed x17, waiting for transfers between devices  126 us
  transfers between devices with their start and end apart: 109, of which 109 were waited for; matrix products, arithmetic and copies ran while one was open for 6% of the time, Pallas kernels for 0%

profile of v1, /device:TPU:0, one launch (start us, length us, event | category | flops | bytes accessed | tf_op | source)
XLA Modules:
  0.0 4465.4 jit_solution(13923830024157500371)
XLA Ops:
  36.0 183.3 %while.86 = (s32[]{:T(128)}, bf16[5,1536,32]{1,2,0:T(8,128)(2,1)}, f32[5,1536]{1,0:T(8,128)}, s32[5]{0:T(128)}, bf16[1536,160]{1,0:T(8,128)(2,1)}, /*index=5*/bf...) while((s32[]{:T(128)}, bf16[5,1536,32]{1,2,0:T(8,128)(2,1)}, ...), condition=%wide.region_9.10_spmd.clone, body=%wide.region_4.9_spmd.clone.sunk | while | flops 107740680 | bytes 11363814 | solution.py:55
  237.3 69.2 %reduce-scatter.19.cloned.1.call-done = f32[1536,160]{0,1:T(8,128)} async-done(((f32[1536,640]{0,1:T(8,128)}), f32[1536,160]{0,1:T(8,128)}) %reduce-scatter.19.cloned.1.call-update) | async-done | bytes 983056 | tf_op jit(solution)/shard_map/reduce_scatter | solution.py:141
  313.8 72.3 %all-gather.8.cloned.1.call-done = f32[1536,640]{0,1:T(8,128)} async-done(((f32[1536,160]{0,1:T(8,128)}), f32[1536,640]{0,1:T(8,128)}) %all-gather.8.cloned.1.call-update) | async-done | bytes 3932176 | tf_op jit(solution)/shard_map/all_gather | solution.py:143
  440.3 2076.3 %while.89 = (s32[]{:T(128)}, f32[160,5120]{1,0:T(8,128)}, f32[160,5120]{1,0:T(8,128)}, f32[12,128,160]{1,0,2:T(8,128)}, s32[12]{0:T(128)S(1)}, /*index=5*/bf16[1...) while((s32[]{:T(128)}, f32[160,5120]{1,0:T(8,128)}, ...), condition=%wide.region_19.20_spmd.clone, body=%wide.region_16.19_spmd.clone.sunk | while | flops 1064796160 | bytes 115196736 | solution.py:200
  501.9 50.8 %reduce-scatter.35.cloned.1.call-done = f32[32,5120]{1,0:T(8,128)} async-done(((f32[128,5120]{1,0:T(8,128)}), f32[32,5120]{1,0:T(8,128)}) %reduce-scatter.35.cloned.1.call-update) | async-done | bytes 655376 | tf_op jit(solution)/shard_map/while/body/eval_jaxpr/reduce_scatter | solution.py:170
  674.8 50.9 %reduce-scatter.35.cloned.1.call-done = f32[32,5120]{1,0:T(8,128)} async-done(((f32[128,5120]{1,0:T(8,128)}), f32[32,5120]{1,0:T(8,128)}) %reduce-scatter.35.cloned.1.call-update) | async-done | bytes 655376 | tf_op jit(solution)/shard_map/while/body/eval_jaxpr/reduce_scatter | solution.py:170
  1193.8 50.8 %reduce-scatter.35.cloned.1.call-done = f32[32,5120]{1,0:T(8,128)} async-done(((f32[128,5120]{1,0:T(8,128)}), f32[32,5120]{1,0:T(8,128)}) %reduce-scatter.35.cloned.1.call-update) | async-done | bytes 655376 | tf_op jit(solution)/shard_map/while/body/eval_jaxpr/reduce_scatter | solution.py:170
  1366.7 50.9 %reduce-scatter.35.cloned.1.call-done = f32[32,5120]{1,0:T(8,128)} async-done(((f32[128,5120]{1,0:T(8,128)}), f32[32,5120]{1,0:T(8,128)}) %reduce-scatter.35.cloned.1.call-update) | async-done | bytes 655376 | tf_op jit(solution)/shard_map/while/body/eval_jaxpr/reduce_scatter | solution.py:170
  2519.2 1148.3 %while.84 = (s32[]{:T(128)}, bf16[12,128,160]{1,2,0:T(8,128)(2,1)}, s32[12]{0:T(128)S(1)}, bf16[1536,160]{1,0:T(8,128)(2,1)}, bf16[160,5120]{1,0:T(8,128)(2,1)},...) while((s32[]{:T(128)}, bf16[12,128,160]{1,2,0:T(8,128)(2,1)}, s32[12]{0:T(128)S(1)}, ...), condition=%wide.region_15.16_spmd, body=%wide.region_13.15_spmd.sunk | while | flops 430080000 | bytes 29638920 | solution.py:160
  2525.4 51.2 %reduce-scatter.33.cloned.1.call-done = f32[32,5120]{1,0:T(8,128)} async-done(((f32[128,5120]{1,0:T(8,128)}), f32[32,5120]{1,0:T(8,128)}) %reduce-scatter.33.cloned.1.call-update) | async-done | bytes 655376 | tf_op jit(solution)/shard_map/while/body/eval_jaxpr/reduce_scatter | solution.py:107
  2621.1 51.2 %reduce-scatter.33.cloned.1.call-done = f32[32,5120]{1,0:T(8,128)} async-done(((f32[128,5120]{1,0:T(8,128)}), f32[32,5120]{1,0:T(8,128)}) %reduce-scatter.33.cloned.1.call-update) | async-done | bytes 655376 | tf_op jit(solution)/shard_map/while/body/eval_jaxpr/reduce_scatter | solution.py:107
  2716.8 51.2 %reduce-scatter.33.cloned.1.call-done = f32[32,5120]{1,0:T(8,128)} async-done(((f32[128,5120]{1,0:T(8,128)}), f32[32,5120]{1,0:T(8,128)}) %reduce-scatter.33.cloned.1.call-update) | async-done | bytes 655376 | tf_op jit(solution)/shard_map/while/body/eval_jaxpr/reduce_scatter | solution.py:107
  2812.5 51.2 %reduce-scatter.33.cloned.1.call-done = f32[32,5120]{1,0:T(8,128)} async-done(((f32[128,5120]{1,0:T(8,128)}), f32[32,5120]{1,0:T(8,128)}) %reduce-scatter.33.cloned.1.call-update) | async-done | bytes 655376 | tf_op jit(solution)/shard_map/while/body/eval_jaxpr/reduce_scatter | solution.py:107
  2908.2 51.2 %reduce-scatter.33.cloned.1.call-done = f32[32,5120]{1,0:T(8,128)} async-done(((f32[128,5120]{1,0:T(8,128)}), f32[32,5120]{1,0:T(8,128)}) %reduce-scatter.33.cloned.1.call-update) | async-done | bytes 655376 | tf_op jit(solution)/shard_map/while/body/eval_jaxpr/reduce_scatter | solution.py:107
  3003.9 51.2 %reduce-scatter.33.cloned.1.call-done = f32[32,5120]{1,0:T(8,128)} async-done(((f32[128,5120]{1,0:T(8,128)}), f32[32,5120]{1,0:T(8,128)}) %reduce-scatter.33.cloned.1.call-update) | async-done | bytes 655376 | tf_op jit(solution)/shard_map/while/body/eval_jaxpr/reduce_scatter | solution.py:107
  3099.6 51.2 %reduce-scatter.33.cloned.1.call-done = f32[32,5120]{1,0:T(8,128)} async-done(((f32[128,5120]{1,0:T(8,128)}), f32[32,5120]{1,0:T(8,128)}) %reduce-scatter.33.cloned.1.call-update) | async-done | bytes 655376 | tf_op jit(solution)/shard_map/while/body/eval_jaxpr/reduce_scatter | solution.py:107
  3195.3 51.2 %reduce-scatter.33.cloned.1.call-done = f32[32,5120]{1,0:T(8,128)} async-done(((f32[128,5120]{1,0:T(8,128)}), f32[32,5120]{1,0:T(8,128)}) %reduce-scatter.33.cloned.1.call-update) | async-done | bytes 655376 | tf_op jit(solution)/shard_map/while/body/eval_jaxpr/reduce_scatter | solution.py:107
  3291.0 51.2 %reduce-scatter.33.cloned.1.call-done = f32[32,5120]{1,0:T(8,128)} async-done(((f32[128,5120]{1,0:T(8,128)}), f32[32,5120]{1,0:T(8,128)}) %reduce-scatter.33.cloned.1.call-update) | async-done | bytes 655376 | tf_op jit(solution)/shard_map/while/body/eval_jaxpr/reduce_scatter | solution.py:107
  3386.6 51.2 %reduce-scatter.33.cloned.1.call-done = f32[32,5120]{1,0:T(8,128)} async-done(((f32[128,5120]{1,0:T(8,128)}), f32[32,5120]{1,0:T(8,128)}) %reduce-scatter.33.cloned.1.call-update) | async-done | bytes 655376 | tf_op jit(solution)/shard_map/while/body/eval_jaxpr/reduce_scatter | solution.py:107
  3482.3 51.2 %reduce-scatter.33.cloned.1.call-done = f32[32,5120]{1,0:T(8,128)} async-done(((f32[128,5120]{1,0:T(8,128)}), f32[32,5120]{1,0:T(8,128)}) %reduce-scatter.33.cloned.1.call-update) | async-done | bytes 655376 | tf_op jit(solution)/shard_map/while/body/eval_jaxpr/reduce_scatter | solution.py:107
  3578.0 51.2 %reduce-scatter.33.cloned.1.call-done = f32[32,5120]{1,0:T(8,128)} async-done(((f32[128,5120]{1,0:T(8,128)}), f32[32,5120]{1,0:T(8,128)}) %reduce-scatter.33.cloned.1.call-update) | async-done | bytes 655376 | tf_op jit(solution)/shard_map/while/body/eval_jaxpr/reduce_scatter | solution.py:107
  3673.1 72.3 %all-gather.16.cloned.1.call-done = f32[1536,640]{0,1:T(8,128)} async-done(((f32[1536,160]{0,1:T(8,128)}), f32[1536,640]{0,1:T(8,128)}) %all-gather.16.cloned.1.call-update) | async-done | bytes 3932176 | tf_op jit(solution)/shard_map/all_gather | solution.py:201
  3801.0 317.2 %while.88 = (s32[]{:T(128)}, bf16[5,1536,32]{2,1,0:T(8,128)(2,1)}, bf16[5,1536,32]{1,2,0:T(8,128)(2,1)}, bf16[5,1536,32]{1,2,0:T(8,128)(2,1)}, s32[5]{0:T(128)},...) while((s32[]{:T(128)}, bf16[5,1536,32]{2,1,0:T(8,128)(2,1)}, ...), condition=%wide.region_26.27_spmd.clone, body=%wide.region_22.26_spmd.clone.sunk | while | flops 259784208 | bytes 27660404 | solution.py:97
  4138.3 67.4 %all-reduce.2.cloned.1.call-done = bf16[1536,640]{0,1:T(8,128)(2,1)} async-done(((bf16[1536,640]{0,1:T(8,128)(2,1)}), bf16[1536,640]{0,1:T(8,128)(2,1)}) %all-reduce.2.cloned.1.call-update) | async-done | bytes 1966096 | tf_op jit(solution)/shard_map/psum | solution.py:220
  (1180 shorter events, 3602.9 us)
Async XLA Ops:
  7.2 299.3 %reduce-scatter.19.cloned.1.call-start = ((), (), s32[]{:S(2)}) async-start(), calls=%async_computation.10 | async-start | bytes 4915200 | tf_op jit(solution)/shard_map/reduce_scatter | solution.py:141
  233.4 152.7 %all-gather.8.cloned.1.call-start = ((), (), s32[]{:S(2)}) async-start(), calls=%async_computation.11 | async-start | bytes 4915200 | tf_op jit(solution)/shard_map/all_gather | solution.py:143
  309.8 130.5 %all-gather.12.cloned.1.call-start = ((), (), s32[]{:S(2)}) async-start(), calls=%async_computation.13 | async-start | bytes 1843200 | tf_op jit(solution)/shard_map/all_gather | solution.py:147
  446.5 106.3 %reduce-scatter.35.cloned.1.call-start = ((), (), s32[]{:S(2)}) async-start(), calls=%async_computation.25 | async-start | bytes 3276800 | tf_op jit(solution)/shard_map/while/body/eval_jaxpr/reduce_scatter | solution.py:170
  449.4 160.5 %all-gather.20.cloned.1.call-start = ((), (), s32[]{:S(2)}) async-start(), calls=%async_computation.27 | async-start | bytes 1638400 | tf_op jit(solution)/shard_map/while/body/eval_jaxpr/all_gather | solution.py:114
  623.3 159.6 %all-gather.20.cloned.1.call-start = ((), (), s32[]{:S(2)}) async-start(), calls=%async_computation.27 | async-start | bytes 1638400 | tf_op jit(solution)/shard_map/while/body/eval_jaxpr/all_gather | solution.py:114
  796.4 159.5 %all-gather.20.cloned.1.call-start = ((), (), s32[]{:S(2)}) async-start(), calls=%async_computation.27 | async-start | bytes 1638400 | tf_op jit(solution)/shard_map/while/body/eval_jaxpr/all_gather | solution.py:114
  969.3 159.5 %all-gather.20.cloned.1.call-start = ((), (), s32[]{:S(2)}) async-start(), calls=%async_computation.27 | async-start | bytes 1638400 | tf_op jit(solution)/shard_map/while/body/eval_jaxpr/all_gather | solution.py:114
  1142.3 159.5 %all-gather.20.cloned.1.call-start = ((), (), s32[]{:S(2)}) async-start(), calls=%async_computation.27 | async-start | bytes 1638400 | tf_op jit(solution)/shard_map/while/body/eval_jaxpr/all_gather | solution.py:114
  1315.2 159.6 %all-gather.20.cloned.1.call-start = ((), (), s32[]{:S(2)}) async-start(), calls=%async_computation.27 | async-start | bytes 1638400 | tf_op jit(solution)/shard_map/while/body/eval_jaxpr/all_gather | solution.py:114
  1488.2 159.5 %all-gather.20.cloned.1.call-start = ((), (), s32[]{:S(2)}) async-start(), calls=%async_computation.27 | async-start | bytes 1638400 | tf_op jit(solution)/shard_map/while/body/eval_jaxpr/all_gather | solution.py:114
  1661.2 159.5 %all-gather.20.cloned.1.call-start = ((), (), s32[]{:S(2)}) async-start(), calls=%async_computation.27 | async-start | bytes 1638400 | tf_op jit(solution)/shard_map/while/body/eval_jaxpr/all_gather | solution.py:114
  1834.1 159.5 %all-gather.20.cloned.1.call-start = ((), (), s32[]{:S(2)}) async-start(), calls=%async_computation.27 | async-start | bytes 1638400 | tf_op jit(solution)/shard_map/while/body/eval_jaxpr/all_gather | solution.py:114
  2007.0 159.5 %all-gather.20.cloned.1.call-start = ((), (), s32[]{:S(2)}) async-start(), calls=%async_computation.27 | async-start | bytes 1638400 | tf_op jit(solution)/shard_map/while/body/eval_jaxpr/all_gather | solution.py:114
  2179.9 159.5 %all-gather.20.cloned.1.call-start = ((), (), s32[]{:S(2)}) async-start(), calls=%async_computation.27 | async-start | bytes 1638400 | tf_op jit(solution)/shard_map/while/body/eval_jaxpr/all_gather | solution.py:114
  2352.8 159.5 %all-gather.20.cloned.1.call-start = ((), (), s32[]{:S(2)}) async-start(), calls=%async_computation.27 | async-start | bytes 1638400 | tf_op jit(solution)/shard_map/while/body/eval_jaxpr/all_gather | solution.py:114
  3668.2 120.7 %all-gather.14.cloned.1.call-start = ((), (), s32[]{:S(2)}) async-start(), calls=%async_computation.14 | async-start | bytes 2457600 | tf_op jit(solution)/shard_map/all_gather | solution.py:161
  3670.2 535.6 %all-reduce.2.cloned.1.call-start = ((), (), s32[]{:S(2)}) async-start(), calls=%async_computation.16 | async-start | bytes 3932160 | tf_op jit(solution)/shard_map/psum | solution.py:220
  4124.8 117.7 %reduce-scatter.31.cloned.1.call-start = ((), (), s32[]{:S(2)}) async-start(), calls=%async_computation.22 | async-start | bytes 737280
  4128.1 155.6 %reduce-scatter.29.cloned.1.call-start = ((), (), s32[]{:S(2)}) async-start(), calls=%async_computation.21 | async-start | bytes 1474560
  4138.2 182.2 %reduce-scatter.27.cloned.1.call-start = ((), (), s32[]{:S(2)}) async-start(), calls=%async_computation.20 | async-start | bytes 368640
  4212.8 144.4 %reduce-scatter.25.cloned.1.call-start = ((), (), s32[]{:S(2)}) async-start(), calls=%async_computation.19 | async-start | bytes 368640
  4213.8 194.1 %reduce-scatter.21.cloned.1.call-start = ((), (), s32[]{:S(2)}) async-start(), calls=%async_computation.17 | async-start | bytes 3686400 | tf_op jit(solution)/shard_map/reduce_scatter | solution.py:203
  4214.4 244.3 %reduce-scatter.23.cloned.1.call-start = ((), (), s32[]{:S(2)}) async-start(), calls=%async_computation.18 | async-start | bytes 3686400 | tf_op jit(solution)/shard_map/reduce_scatter | solution.py:204
  (187 other events, 6364.6 us)
Sparse Core Ops, SparseCore 0:
  233.5 72.9 reduce-scatter.18
  309.2 76.8 all-gather.7
  446.6 52.0 reduce-scatter.36
  500.9 51.7 reduce-scatter.34
  620.5 51.0 reduce-scatter.36
  674.0 51.7 reduce-scatter.34
  793.6 51.1 reduce-scatter.36
  846.9 51.7 reduce-scatter.34
  966.5 51.0 reduce-scatter.36
  1019.8 51.7 reduce-scatter.34
  1192.8 51.7 reduce-scatter.34
  1365.8 51.7 reduce-scatter.34
  1485.4 51.0 reduce-scatter.36
  1538.7 51.7 reduce-scatter.34
  1658.4 51.1 reduce-scatter.36
  1711.7 51.7 reduce-scatter.34
  1884.5 51.7 reduce-scatter.34
  2057.5 51.7 reduce-scatter.34
  2177.1 51.1 reduce-scatter.36
  2230.4 51.7 reduce-scatter.34
  2403.3 51.7 reduce-scatter.34
  2908.3 51.0 reduce-scatter.32
  3669.9 75.4 all-gather.15
  4124.9 80.7 all-reduce.1
  (49 shorter events, 1937.3 us)
